TPU v7x, 512 devices: a whole 4x8x8 slice. The times are simulated.
512 devices in a mesh: seq: 32 (over x, y), dp: 8 (over z), domain: 2 (over core).
Axes of the slice: x: 4, y: 8, z: 8, core: 2. Of those that a mesh axis runs over, the one named last changes fastest.
Arguments:
- history: bfloat16 [2, 8, 8192, 1024], P('domain', 'dp', 'seq'), may hold values from -6 to 6
- qkv_weight: bfloat16 [2, 1024, 3072], P('domain', 'seq'), may hold values from -0.375 to 0.375
- norm_gain: float32 [2, 1024], P('domain'), may hold values from 0.1 to 1.9
- pool_gain: float32 [2, 1024], P('domain'), may hold values from 0.1 to 1.9
- lengths: int32 [2, 8], P('domain', 'dp'), may hold values from 1024 to 8192, as said below
- positives: int32 [8], replicated, may hold values from 0 to 7, each once
Outputs:
- user_vec: bfloat16 [2, 8, 1024], P('domain', 'dp', 'seq')
- loss: float32 [2, 8], P('domain', 'dp')
Inputs may be any that keep to these rules, and one draw needn't show every extreme that they name: `lengths`: in each domain one user has exactly 8192 valid events and another exactly 1024. `positives`: each user of the second domain is named exactly once.
All inputs are finite; a program needn't handle non-finite values.
Results may differ from a plain program's by a relative error of at most 0.0085.
Values may be sent and summed in bfloat16 or wider, within the bound.
A program may use at most 64 MiB of HBM per device.

v0:
```python
import jax
import jax.numpy as jnp
from jax import lax
from jax.sharding import PartitionSpec as P

HEADS = 8
HEAD_DIM = 128
logit_scale = 20.0
epsilon = 1e-06
highest = lax.Precision.HIGHEST


def carried_in(part, axis, combine, identity):
    place = lax.axis_index(axis)
    gathered = jax.tree.map(lambda a: lax.all_gather(a, axis), part)
    state = jax.tree.map(lambda a, e: jnp.zeros_like(a) + jnp.asarray(e, a.dtype), part, identity)

    def one(hop, state):
        return combine(
            state, jax.tree.map(lambda a: lax.dynamic_index_in_dim(a, hop, 0, False), gathered)
        )

    return lax.fori_loop(0, place, one, state)


def partner_2(block, axis, stride):
    count = lax.axis_size(axis)
    route = []
    for low in range(count):
        high = low | 1 << stride
        if high != low and high < count:
            route += [(low, high), (high, low)]
    return lax.ppermute(block, axis, route)


def feature_map(values):
    return jax.nn.elu(values) + 1.0


def add_pair(earlier, later):
    return (earlier[0] + later[0], earlier[1] + later[1])


def shards(history, qkv_weight, norm_gain, pool_gain, lengths, positives):
    seq_count = lax.axis_size("seq")
    seq_place = lax.axis_index("seq")
    group_place = lax.axis_index("dp")
    domain_place = lax.axis_index("domain")
    events = history[0]
    users_dev, tokens_dev, width = events.shape
    row_count = users_dev * tokens_dev
    wide = events.astype(jnp.float32)
    normed = (
        wide * lax.rsqrt(jnp.mean(wide * wide, -1, keepdims=True) + epsilon) * norm_gain[0]
    ).astype(jnp.bfloat16)
    normed = normed.reshape(row_count, width)
    rows_here = qkv_weight[0]

    def add_rows(piece):
        return jnp.dot(normed, piece, preferred_element_type=jnp.float32)

    query_raw = add_rows(lax.all_gather(rows_here[:, :width], "seq", axis=0, tiled=True))
    key_raw = add_rows(lax.all_gather(rows_here[:, width : 2 * width], "seq", axis=0, tiled=True))
    value_raw = add_rows(lax.all_gather(rows_here[:, 2 * width :], "seq", axis=0, tiled=True))
    positions = seq_place * tokens_dev + jnp.arange(tokens_dev)
    valid = positions[None, :] < lengths[0][:, None]
    shape_heads = (users_dev, tokens_dev, HEADS, HEAD_DIM)
    queries = feature_map(query_raw).astype(jnp.bfloat16).reshape(shape_heads)
    key_feats = (
        jnp.where(valid.reshape(row_count)[:, None], feature_map(key_raw), 0.0)
        .astype(jnp.bfloat16)
        .reshape(shape_heads)
    )
    val_feats = value_raw.astype(jnp.bfloat16).reshape(shape_heads)
    local_state = jnp.einsum(
        "uthc,uthd->uhcd", key_feats, val_feats, preferred_element_type=jnp.float32
    )
    local_total = jnp.sum(key_feats.astype(jnp.float32), axis=1)
    state_before, total_before = carried_in(
        (local_state, local_total),
        "seq",
        add_pair,
        (jnp.zeros_like(local_state), jnp.zeros_like(local_total)),
    )
    causal = jnp.arange(tokens_dev)[:, None] >= jnp.arange(tokens_dev)[None, :]
    scores = jnp.einsum("uthc,ushc->uhts", queries, key_feats, preferred_element_type=jnp.float32)
    scores = jnp.where(causal, scores, 0.0)
    denominator = jnp.sum(scores, axis=-1) + jnp.einsum(
        "uthc,uhc->uht", queries.astype(jnp.float32), total_before, precision=highest
    )
    numerator = jnp.einsum(
        "uhts,ushc->uthc",
        scores.astype(jnp.bfloat16),
        val_feats,
        preferred_element_type=jnp.float32,
    )
    numerator = numerator + jnp.einsum(
        "uthc,uhcd->uthd",
        queries,
        state_before.astype(jnp.bfloat16),
        preferred_element_type=jnp.float32,
    )
    attended = numerator / jnp.transpose(denominator, (0, 2, 1))[..., None]
    attended = attended.reshape(users_dev, tokens_dev, width)
    partial_value = jnp.sum(jnp.where(valid[..., None], wide + attended, 0.0), axis=1)
    piece_width = width // seq_count
    gain_row = pool_gain[0]
    pooled = lax.psum(partial_value, "seq")
    factor = lax.rsqrt(jnp.mean(pooled * pooled, -1, keepdims=True) + epsilon)
    full_vec = (pooled * factor * gain_row).astype(jnp.bfloat16)
    out_vec = lax.dynamic_slice_in_dim(full_vec, seq_place * piece_width, piece_width, 1)
    group = lax.all_gather(full_vec, "dp", axis=0, tiled=True)
    other = partner_2(group, "domain", 0)
    logits = jnp.einsum("uc,vc->uv", full_vec, other, preferred_element_type=jnp.float32) * (
        logit_scale / width
    )
    users_all = other.shape[0]
    own_index = group_place * users_dev + jnp.arange(users_dev)
    targets = lax.dynamic_slice_in_dim(positives, group_place * users_dev, users_dev)
    forward_pair = targets[:, None] == jnp.arange(users_all)[None, :]
    backward_pair = positives[None, :] == own_index[:, None]
    partner = jnp.where(domain_place == 0, forward_pair, backward_pair)
    loss = jnp.log(jnp.sum(jnp.exp(logits), axis=-1)) - jnp.sum(
        jnp.where(partner, logits, 0.0), axis=-1
    )
    return (out_vec[None], loss[None])


def solution(mesh):
    placed = (
        P("domain", "dp", "seq", None),
        P("domain", "seq", None),
        P("domain", None),
        P("domain", None),
        P("domain", "dp"),
        P(),
    )
    return jax.shard_map(
        shards,
        mesh=mesh,
        in_specs=placed,
        out_specs=(P("domain", "dp", "seq"), P("domain", "dp")),
        check_vma=False,
    )
```

profile of v0, /device:TPU:1, one launch (start us, length us, event | category | flops | bytes accessed | tf_op | source)
XLA Modules:
  0.0 566.4 jit_solution(12575679889314143297)
XLA Ops:
  7.2 0.0 all-gather.11.cloned.1.call-start
  7.2 1.6 fusion.51
  8.8 0.0 all-gather.11.cloned.1.call-update
  8.8 0.0 all-gather.7.cloned.1.call-start
  8.9 0.7 all-gather.7.cloned.1.call-update
  9.6 0.0 all-gather.9.cloned.1.call-start
  9.6 0.7 all-gather.9.cloned.1.call-update
  10.3 0.0 all-gather.13.cloned.1.call-start
  11.0 1.2 fusion.5
  12.2 82.9 %all-gather.11.cloned.1.call-done = bf16[1024,1024]{1,0:T(8,128)(2,1)} async-done(((bf16[32,1024]{1,0:T(8,128)(2,1)}), bf16[1024,1024]{1,0:T(8,128)(2,1)}) %all-gather.11.cloned.1.call-update) | async-done | bytes 2097168 | tf_op jit(solution)/shard_map/all_gather | solution.py:63
  95.1 0.0 copy-start
  95.1 0.0 copy-start.2
  95.1 3.0 convert_reduce_fusion
  98.1 0.2 copy.43
  98.3 0.0 copy-start.3
  98.3 80.6 %all-gather.7.cloned.1.call-done = bf16[1024,1024]{1,0:T(8,128)(2,1)} async-done(((bf16[32,1024]{1,0:T(8,128)(2,1)}), bf16[1024,1024]{1,0:T(8,128)(2,1)}) %all-gather.7.cloned.1.call-update) | async-done | bytes 2097168 | tf_op jit(solution)/shard_map/all_gather | solution.py:64
  178.9 0.0 copy-done
  178.9 0.0 copy-done.2
  178.9 2.4 fusion.3
  181.3 1.1 fusion.29
  182.4 0.0 all-gather.13.cloned.1.call-update
  182.4 0.0 copy-done.3
  182.4 0.7 dynamic_slice.15
  183.1 31.5 %all_gather.30 = f32[32,1,8,128]{3,2,1,0:T(8,128)S(1)} all-gather(f32[1,1,8,128]{3,2,1,0:T(8,128)S(1)} %bitcast.122), channel_id=1, replica_groups=mesh['seq'=32,'dp'=8,'domain'=2] {'seq'}, dimensions={0}, use_global_device_ids=true | all-gather | bytes 135168 | tf_op jit(solution)/shard_map/all_gather | solution.py:15
  214.6 48.1 %all-gather.9.cloned.1.call-done = bf16[1024,1024]{1,0:T(8,128)(2,1)} async-done(((bf16[32,1024]{1,0:T(8,128)(2,1)}), bf16[1024,1024]{1,0:T(8,128)(2,1)}) %all-gather.9.cloned.1.call-update) | async-done | bytes 2097168 | tf_op jit(solution)/shard_map/all_gather | solution.py:62
  262.7 2.7 fusion.22
  265.4 0.0 copy-start.4
  265.4 0.5 select_reduce_fusion
  266.0 0.4 fusion.11
  266.3 145.7 %all-gather.13.cloned.1.call-done = f32[256,128,128]{2,1,0:T(8,128)} async-done(((f32[8,128,128]{2,1,0:T(8,128)}), f32[256,128,128]{2,1,0:T(8,128)}) %all-gather.13.cloned.1.call-update) | async-done | bytes 16777232 | tf_op jit(solution)/shard_map/all_gather | solution.py:15
  412.1 0.0 copy-done.4
  412.1 0.5 fusion.24
  412.6 1.4 fusion.21
  414.0 0.0 copy-start.1
  414.0 0.3 copy.37
  414.3 0.2 fusion.7
  414.6 94.9 %psum.7 = f32[1,1024]{1,0:T(1,128)S(1)} all-reduce(f32[1,1024]{1,0:T(1,128)S(1)} %bitcast.119), channel_id=1, replica_groups=mesh['seq'=32,'dp'=8,'domain'=2] {'seq'}, use_global_device_ids=true, to_apply=%region_6.7 | all-reduce | flops 1024 | bytes 8192 | tf_op jit(solution)/shard_map/psum | solution.py:108
  509.5 0.6 multiply_reduce_fusion
  510.8 0.0 copy-done.1
  510.8 20.9 %all-gather.1 = bf16[8,1,1024]{2,1,0:T(2,128)(2,1)S(1)} all-gather(bf16[1,1,1024]{2,1,0:T(2,128)(2,1)S(1)} %bitcast.121), channel_id=1, replica_groups=mesh['seq'=32,'dp'=8,'domain'=2] {'dp'}, dimensions={0}, use_global_device_ids=true | all-gather | bytes 18432 | tf_op jit(solution)/shard_map/all_gather | solution.py:112
  531.7 23.3 %collective-permute-start = (bf16[8,1024]{1,0:T(8,128)(2,1)S(1)}, bf16[8,1024]{1,0:T(8,128)(2,1)S(1)}, u32[]{:S(2)}, u32[]{:S(2)}) collective-permute-start(bf16[8,1024]{1,0:T(8,128)(2,1)S(1)} %bitcast.120), channel_id=1, source_target_pairs={{0,1},{1,0},{2,3},{3,2},{4,5},{5,4},{6,7},{7,6},{8,9},{9,8},{10,11... | collective-permute-start | bytes 49160 | tf_op jit(solution)/shard_map/ppermute | solution.py:33
  555.0 0.6 dynamic-slice_bitcast_fusion
  555.6 0.2 collective-permute-done
  555.8 1.5 fusion.40
  (9 shorter events, 0.1 us)
Async XLA Ops:
  7.2 87.9 %all-gather.11.cloned.1.call-start = ((), (), s32[]{:S(2)}) async-start(), calls=%async_computation.2 | async-start | bytes 2162688 | tf_op jit(solution)/shard_map/all_gather | solution.py:63
  8.8 170.1 %all-gather.7.cloned.1.call-start = ((), (), s32[]{:S(2)}) async-start(), calls=%async_computation | async-start | bytes 2162688 | tf_op jit(solution)/shard_map/all_gather | solution.py:64
  9.6 253.1 %all-gather.9.cloned.1.call-start = ((), (), s32[]{:S(2)}) async-start(), calls=%async_computation.1 | async-start | bytes 2162688 | tf_op jit(solution)/shard_map/all_gather | solution.py:62
  10.3 401.7 %all-gather.13.cloned.1.call-start = ((), (), s32[]{:S(2)}) async-start(), calls=%async_computation.3 | async-start | bytes 17301504 | tf_op jit(solution)/shard_map/all_gather | solution.py:15
  95.1 83.8 %copy-start = (bf16[1,1,256,1024]{3,2,1,0:T(8,128)(2,1)S(1)}, bf16[1,1,256,1024]{3,2,1,0:T(8,128)(2,1)}, u32[]{:S(2)}) copy-start(bf16[1,1,256,1024]{3,2,1,0:T(8,128)(2,1)} %param.8) | copy-start | bytes 1572868
  95.1 83.8 %copy-start.2 = (f32[1,1024]{1,0:T(1,128)S(1)}, f32[1,1024]{1,0:T(1,128)}, u32[]{:S(2)}) copy-start(f32[1,1024]{1,0:T(1,128)} %param.10) | copy-start | bytes 12292
  98.3 84.1 %copy-start.3 = (s32[8]{0:T(128)S(1)}, s32[8]{0:T(128)}, u32[]{:S(2)}) copy-start(s32[8]{0:T(128)} %param.13) | copy-start | bytes 100
  265.4 146.6 %copy-start.4 = (bf16[32,8,8,128]{3,2,1,0:T(8,128)(2,1)}, bf16[32,8,8,128]{3,2,1,0:T(8,128)(2,1)S(1)}, u32[]{:S(2)}) copy-start(bf16[32,8,8,128]{3,2,1,0:T(8,128)(2,1)S(1)} %fusion.22) | copy-start | bytes 1572868
  414.0 96.8 %copy-start.1 = (f32[1,1024]{1,0:T(1,128)S(1)}, f32[1,1024]{1,0:T(1,128)}, u32[]{:S(2)}) copy-start(f32[1,1024]{1,0:T(1,128)} %param.11) | copy-start | bytes 12292
  531.7 24.1 %collective-permute-start = (bf16[8,1024]{1,0:T(8,128)(2,1)S(1)}, bf16[8,1024]{1,0:T(8,128)(2,1)S(1)}, u32[]{:S(2)}, u32[]{:S(2)}) collective-permute-start(bf16[8,1024]{1,0:T(8,128)(2,1)S(1)} %bitcast.120), channel_id=1, source_target_pairs={{0,1},{1,0},{2,3},{3,2},{4,5},{5,4},{6,7},{7,6},{8,9},{9,8},{10,11... | collective-permute-start | bytes 49160 | tf_op jit(solution)/shard_map/ppermute | solution.py:33
Sparse Core Ops, SparseCore 0:
  11.1 83.9 all-gather.10
  98.3 80.6 all-gather.6
  182.1 80.5 all-gather.8
  265.7 146.2 all-gather.12
where the time goes:
time: 568 us; the launch traced here: 566 us
  waiting for transfers between devices  359 us (63%)
  blocking collectives  147 us (26%)
  starting transfers between devices  23.4 us (4%)
  between operations  17.8 us (3%)
  matrix products  13.5 us (2%)
    all_gather x1, waiting for transfers between devices, carried_in(): gathered = jax.tree.map(lambda a: lax.all_gather(a, axis), part)  146 us
    psum x1, blocking collectives, shards(): pooled = lax.psum(partial_value, 'seq')  94.9 us
    all_gather x1, waiting for transfers between devices, shards(): lax.all_gather(rows_here[:, width:2 * width], 'seq', axis=0, tiled=True)  82.9 us
    all_gather x1, waiting for transfers between devices, shards(): lax.all_gather(rows_here[:, 2 * width:], 'seq', axis=0, tiled=True)  80.6 us
    all_gather x1, waiting for transfers between devices, shards(): lax.all_gather(rows_here[:, :width], 'seq', axis=0, tiled=True)  48.1 us
    all_gather x1, blocking collectives, carried_in(): gathered = jax.tree.map(lambda a: lax.all_gather(a, axis), part)  31.5 us
    ppermute x1, starting transfers between devices, partner_2(): return lax.ppermute(block, axis, route)  23.3 us
    all_gather x1, blocking collectives, shards(): group = lax.all_gather(full_vec, 'dp', axis=0, tiled=True)  20.9 us
  transfers between devices with their start and end apart: 5, of which 5 were waited for; matrix products, arithmetic and copies ran while one was open for 2% of the time, Pallas kernels for 0%

commit v1 on v0

--- a/solution.py
+++ b/solution.py
@@ -105,7 +105,7 @@
     partial_value = jnp.sum(jnp.where(valid[..., None], wide + attended, 0.0), axis=1)
     piece_width = width // seq_count
     gain_row = pool_gain[0]
-    pooled = lax.psum(partial_value, "seq")
+    pooled = lax.all_gather(partial_value, "seq").sum(axis=0)
     factor = lax.rsqrt(jnp.mean(pooled * pooled, -1, keepdims=True) + epsilon)
     full_vec = (pooled * factor * gain_row).astype(jnp.bfloat16)
     out_vec = lax.dynamic_slice_in_dim(full_vec, seq_place * piece_width, piece_width, 1)

time: 568 us -> 533 us (0.938)
  blocking collectives: 147 us -> 117 us
    psum x1 -> x0, blocking collectives: 94.9 us -> none  [shards(): pooled = lax.psum(partial_value, 'seq')]
    all_gather x0 -> x1, blocking collectives: none -> 65.2 us  [shards(): pooled = lax.all_gather(partial_value, 'seq').sum(axis=0)]
where the time goes in v1:
time: 533 us; the launch traced here: 531 us
  waiting for transfers between devices  359 us (67%)
  blocking collectives  117 us (22%)
  starting transfers between devices  18.2 us (3%)
  between operations  17.8 us (3%)
  matrix products  13.5 us (3%)
    all_gather x1, waiting for transfers between devices, carried_in(): gathered = jax.tree.map(lambda a: lax.all_gather(a, axis), part)  146 us
    all_gather x1, waiting for transfers between devices, shards(): lax.all_gather(rows_here[:, width:2 * width], 'seq', axis=0, tiled=True)  82.9 us
    all_gather x1, waiting for transfers between devices, shards(): lax.all_gather(rows_here[:, 2 * width:], 'seq', axis=0, tiled=True)  80.6 us
    all_gather x1, blocking collectives, shards(): pooled = lax.all_gather(partial_value, 'seq').sum(axis=0)  65.2 us
    all_gather x1, waiting for transfers between devices, shards(): lax.all_gather(rows_here[:, :width], 'seq', axis=0, tiled=True)  48.1 us
    all_gather x1, blocking collectives, carried_in(): gathered = jax.tree.map(lambda a: lax.all_gather(a, axis), part)  31.5 us
    all_gather x1, blocking collectives, shards(): group = lax.all_gather(full_vec, 'dp', axis=0, tiled=True)  20.5 us
    ppermute x1, starting transfers between devices, partner_2(): return lax.ppermute(block, axis, route)  18 us
  transfers between devices with their start and end apart: 5, of which 5 were waited for; matrix products, arithmetic and copies ran while one was open for 2% of the time, Pallas kernels for 0%

profile of v1, /device:TPU:1, one launch (start us, length us, event | category | flops | bytes accessed | tf_op | source)
XLA Modules:
  0.0 531.1 jit_solution(3756560640286931976)
XLA Ops:
  7.2 0.0 all-gather.12.cloned.1.call-start
  7.2 1.6 fusion.51
  8.8 0.0 all-gather.12.cloned.1.call-update
  8.8 0.0 all-gather.8.cloned.1.call-start
  8.9 0.7 all-gather.8.cloned.1.call-update
  9.6 0.0 all-gather.10.cloned.1.call-start
  9.6 0.7 all-gather.10.cloned.1.call-update
  10.3 0.0 all-gather.14.cloned.1.call-start
  11.0 1.2 fusion.5
  12.2 82.9 %all-gather.12.cloned.1.call-done = bf16[1024,1024]{1,0:T(8,128)(2,1)} async-done(((bf16[32,1024]{1,0:T(8,128)(2,1)}), bf16[1024,1024]{1,0:T(8,128)(2,1)}) %all-gather.12.cloned.1.call-update) | async-done | bytes 2097168 | tf_op jit(solution)/shard_map/all_gather | solution.py:63
  95.1 0.0 copy-start
  95.1 0.0 copy-start.2
  95.1 3.0 convert_reduce_fusion
  98.1 0.2 copy.53
  98.3 0.0 copy-start.3
  98.3 80.6 %all-gather.8.cloned.1.call-done = bf16[1024,1024]{1,0:T(8,128)(2,1)} async-done(((bf16[32,1024]{1,0:T(8,128)(2,1)}), bf16[1024,1024]{1,0:T(8,128)(2,1)}) %all-gather.8.cloned.1.call-update) | async-done | bytes 2097168 | tf_op jit(solution)/shard_map/all_gather | solution.py:64
  178.9 0.0 copy-done
  178.9 0.0 copy-done.2
  178.9 2.4 fusion.3
  181.3 1.1 fusion.29
  182.4 0.0 all-gather.14.cloned.1.call-update
  182.4 0.0 copy-done.3
  182.4 0.7 dynamic_slice.15
  183.1 31.5 %all_gather.36 = f32[32,1,8,128]{3,2,1,0:T(8,128)S(1)} all-gather(f32[1,1,8,128]{3,2,1,0:T(8,128)S(1)} %bitcast.122), channel_id=1, replica_groups=mesh['seq'=32,'dp'=8,'domain'=2] {'seq'}, dimensions={0}, use_global_device_ids=true | all-gather | bytes 135168 | tf_op jit(solution)/shard_map/all_gather | solution.py:15
  214.6 48.1 %all-gather.10.cloned.1.call-done = bf16[1024,1024]{1,0:T(8,128)(2,1)} async-done(((bf16[32,1024]{1,0:T(8,128)(2,1)}), bf16[1024,1024]{1,0:T(8,128)(2,1)}) %all-gather.10.cloned.1.call-update) | async-done | bytes 2097168 | tf_op jit(solution)/shard_map/all_gather | solution.py:62
  262.7 2.7 fusion.22
  265.4 0.0 copy-start.4
  265.4 0.5 select_reduce_fusion
  266.0 0.4 fusion.11
  266.3 145.7 %all-gather.14.cloned.1.call-done = f32[256,128,128]{2,1,0:T(8,128)} async-done(((f32[8,128,128]{2,1,0:T(8,128)}), f32[256,128,128]{2,1,0:T(8,128)}) %all-gather.14.cloned.1.call-update) | async-done | bytes 16777232 | tf_op jit(solution)/shard_map/all_gather | solution.py:15
  412.1 0.0 copy-done.4
  412.1 0.5 fusion.24
  412.6 1.4 fusion.21
  414.0 0.0 copy-start.1
  414.0 0.3 copy.47
  414.3 0.2 fusion.7
  414.6 65.2 %all-gather.1 = f32[32768]{0:T(1024)S(1)} all-gather(f32[1024]{0:T(1024)S(1)} %fusion.7), channel_id=3, replica_groups=mesh['seq'=32,'dp'=8,'domain'=2] {'seq'}, dimensions={0}, use_global_device_ids=true | all-gather | bytes 135168 | tf_op jit(solution)/shard_map/all_gather | solution.py:108
  479.8 0.6 multiply_reduce_fusion
  481.1 0.0 copy-done.1
  481.1 20.5 %all-gather.2 = bf16[8,1,1024]{2,1,0:T(2,128)(2,1)S(1)} all-gather(bf16[1,1,1024]{2,1,0:T(2,128)(2,1)S(1)} %bitcast.120), channel_id=1, replica_groups=mesh['seq'=32,'dp'=8,'domain'=2] {'dp'}, dimensions={0}, use_global_device_ids=true | all-gather | bytes 18432 | tf_op jit(solution)/shard_map/all_gather | solution.py:112
  501.7 18.0 %collective-permute-start = (bf16[8,1024]{1,0:T(8,128)(2,1)S(1)}, bf16[8,1024]{1,0:T(8,128)(2,1)S(1)}, u32[]{:S(2)}, u32[]{:S(2)}) collective-permute-start(bf16[8,1024]{1,0:T(8,128)(2,1)S(1)} %bitcast.119), channel_id=1, source_target_pairs={{0,1},{1,0},{2,3},{3,2},{4,5},{5,4},{6,7},{7,6},{8,9},{9,8},{10,11... | collective-permute-start | bytes 49160 | tf_op jit(solution)/shard_map/ppermute | solution.py:33
  519.7 0.6 dynamic-slice_bitcast_fusion
  520.3 0.2 collective-permute-done
  520.5 1.5 fusion.40
  (12 shorter events, 0.2 us)
Async XLA Ops:
  7.2 87.9 %all-gather.12.cloned.1.call-start = ((), (), s32[]{:S(2)}) async-start(), calls=%async_computation.2 | async-start | bytes 2162688 | tf_op jit(solution)/shard_map/all_gather | solution.py:63
  8.8 170.1 %all-gather.8.cloned.1.call-start = ((), (), s32[]{:S(2)}) async-start(), calls=%async_computation | async-start | bytes 2162688 | tf_op jit(solution)/shard_map/all_gather | solution.py:64
  9.6 253.1 %all-gather.10.cloned.1.call-start = ((), (), s32[]{:S(2)}) async-start(), calls=%async_computation.1 | async-start | bytes 2162688 | tf_op jit(solution)/shard_map/all_gather | solution.py:62
  10.3 401.7 %all-gather.14.cloned.1.call-start = ((), (), s32[]{:S(2)}) async-start(), calls=%async_computation.3 | async-start | bytes 17301504 | tf_op jit(solution)/shard_map/all_gather | solution.py:15
  95.1 83.8 %copy-start = (bf16[1,1,256,1024]{3,2,1,0:T(8,128)(2,1)S(1)}, bf16[1,1,256,1024]{3,2,1,0:T(8,128)(2,1)}, u32[]{:S(2)}) copy-start(bf16[1,1,256,1024]{3,2,1,0:T(8,128)(2,1)} %param.8) | copy-start | bytes 1572868
  95.1 83.8 %copy-start.2 = (f32[1,1024]{1,0:T(1,128)S(1)}, f32[1,1024]{1,0:T(1,128)}, u32[]{:S(2)}) copy-start(f32[1,1024]{1,0:T(1,128)} %param.10) | copy-start | bytes 12292
  98.3 84.1 %copy-start.3 = (s32[8]{0:T(128)S(1)}, s32[8]{0:T(128)}, u32[]{:S(2)}) copy-start(s32[8]{0:T(128)} %param.13) | copy-start | bytes 100
  265.4 146.6 %copy-start.4 = (bf16[32,8,8,128]{3,2,1,0:T(8,128)(2,1)}, bf16[32,8,8,128]{3,2,1,0:T(8,128)(2,1)S(1)}, u32[]{:S(2)}) copy-start(bf16[32,8,8,128]{3,2,1,0:T(8,128)(2,1)S(1)} %fusion.22) | copy-start | bytes 1572868
  414.0 67.1 %copy-start.1 = (f32[1,1024]{1,0:T(1,128)S(1)}, f32[1,1024]{1,0:T(1,128)}, u32[]{:S(2)}) copy-start(f32[1,1024]{1,0:T(1,128)} %param.11) | copy-start | bytes 12292
  501.7 18.8 %collective-permute-start = (bf16[8,1024]{1,0:T(8,128)(2,1)S(1)}, bf16[8,1024]{1,0:T(8,128)(2,1)S(1)}, u32[]{:S(2)}, u32[]{:S(2)}) collective-permute-start(bf16[8,1024]{1,0:T(8,128)(2,1)S(1)} %bitcast.119), channel_id=1, source_target_pairs={{0,1},{1,0},{2,3},{3,2},{4,5},{5,4},{6,7},{7,6},{8,9},{9,8},{10,11... | collective-permute-start | bytes 49160 | tf_op jit(solution)/shard_map/ppermute | solution.py:33
Sparse Core Ops, SparseCore 0:
  11.1 83.9 all-gather.11
  98.3 80.6 all-gather.7
  182.1 80.5 all-gather.9
  265.7 146.2 all-gather.13
